TPU v7x, 256 devices: a whole 4x4x8 slice. The times are simulated.
256 devices in a mesh: sector: 128 (over z, y_lo, x, core), blk: 2 (over y_hi).
Axes of the slice: x: 4, y: 4 (y_hi: 2, y_lo: 2; y = y_hi * 2 + y_lo), z: 8, core: 2. Of those that a mesh axis runs over, the one named last changes fastest.
Arguments:
- signal: bfloat16 [4, 4096, 8192], P('blk', 'sector'), may hold values from -6 to 6
- offsets: int32 [4], P('blk'), may hold values from 0 to 4095
- fraction: float32 [4, 8192], P('blk'), may hold values from 0 to 1
- radius: float32 [256], replicated, may hold values from 0.2 to 0.9
- azimuth: float32 [256], replicated, may hold values from -3.140625 to 3.140625
Outputs:
- power: float32 [512, 256], P(('sector', 'blk'))
All inputs are finite; a program needn't handle non-finite values.
Results may differ from a plain program's by a relative error of at most 0.00095.
Values may be sent and summed in bfloat16 or wider, within the bound.
No kernel may reach another device: no remote copies, remote signals or barrier semaphores. Data moves between devices by JAX's collectives and lax.ppermute only.
A program may use at most 64 MiB of HBM per device.

v0:
```python
import math
import jax
import jax.numpy as jnp
from jax import lax
from jax.sharding import PartitionSpec as P

NFFT = 1024
wavenumber = 2.0
height = 0.5


def from_behind(x, axis, by):
    size = lax.axis_size(axis)
    return lax.ppermute(x, axis, [(i, (i + by) % size) for i in range(size)])


def fourier_table(groups):
    half_bins = NFFT // 2
    per_group = half_bins // groups
    sample = lax.iota(jnp.int32, NFFT)[:, None]
    column = lax.iota(jnp.int32, 2 * half_bins)[None, :]
    group = column // (2 * per_group)
    part = column // per_group % 2
    inner = column % per_group
    frequency = group * per_group + inner
    turns = (sample * frequency % NFFT).astype(jnp.float32)
    angle = turns * (2.0 * math.pi / NFFT)
    window = 0.5 - 0.5 * jnp.cos(sample.astype(jnp.float32) * (2.0 * math.pi / NFFT))
    value = jnp.where(part == 0, jnp.cos(angle), -jnp.sin(angle))
    return (value * window / math.sqrt(3.0 * NFFT / 8.0)).astype(jnp.bfloat16)


def distances(radius, azimuth, total_mics):
    turn = lax.iota(jnp.int32, total_mics).astype(jnp.float32) * (2.0 * math.pi / total_mics)
    cycle_cos = jnp.cos(turn)[:, None]
    cycle_sin = jnp.sin(turn)[:, None]
    across = (radius * jnp.cos(azimuth))[None, :]
    along = (radius * jnp.sin(azimuth))[None, :]
    squared = (
        1.0
        + height * height
        + (radius * radius)[None, :]
        - 2.0 * (cycle_cos * across + cycle_sin * along)
    )
    return jnp.sqrt(squared)


def steering(frequency, distance):
    phase = wavenumber * frequency.astype(jnp.float32) * distance
    return jnp.concatenate([jnp.cos(phase), jnp.sin(phase)], 1).astype(jnp.bfloat16)


def interpolate(window_rows, weight):
    lower = window_rows[:, :-1].astype(jnp.float32)
    upper = window_rows[:, 1:].astype(jnp.float32)
    spread_weight = weight[:, None, :]
    return ((1.0 - spread_weight) * lower + spread_weight * upper).astype(jnp.bfloat16)


def segment_spectra(virtual, table):
    blocks, mics, length = virtual.shape
    half = NFFT // 2
    halves = virtual.reshape(blocks, mics, length // half, half)
    upper = jnp.einsum(
        "bmhn,nc->bhcm", halves[:, :, :-1], table[:half], preferred_element_type=jnp.float32
    )
    lower = jnp.einsum(
        "bmhn,nc->bhcm", halves[:, :, 1:], table[half:], preferred_element_type=jnp.float32
    )
    return (upper + lower).astype(jnp.bfloat16)


def band_power(flat, first, count, distance):
    snapshots = flat.shape[0]
    points = distance.shape[1]

    def one_bin(bin_place):
        picked = lax.dynamic_index_in_dim(flat, bin_place, 2, keepdims=False)
        stacked = jnp.concatenate([picked[:, 0], picked[:, 1]], 0)
        steer = steering(first + bin_place, distance)
        product = jnp.dot(stacked, steer, preferred_element_type=jnp.float32)
        along = product[:snapshots, :points] + product[snapshots:, points:]
        across = product[snapshots:, :points] - product[:snapshots, points:]
        return jnp.sum(along * along + across * across, 0)

    return lax.map(one_bin, jnp.arange(count, dtype=jnp.int32))


def local(signal, offsets, fraction, radius, azimuth):
    blocks, mics, length = signal.shape
    sectors = lax.axis_size("sector")
    sector_index = lax.axis_index("sector")
    total_mics = mics * sectors
    hop_count = offsets // mics
    within = offsets % mics
    current = signal
    for place in range((sectors - 1).bit_length()):
        moved = from_behind(current, "sector", -(1 << place))
        chosen = hop_count // (1 << place) % 2 == 1
        current = jnp.where(chosen[:, None, None], moved, current)
    following = from_behind(current, "sector", -1)
    joined = jnp.concatenate([current, following], 1)
    window_rows = jax.vmap(lambda rows, start: lax.dynamic_slice_in_dim(rows, start, mics + 1, 0))(
        joined, within
    )
    virtual = interpolate(window_rows, fraction)
    spectra = segment_spectra(virtual, fourier_table(sectors))
    banded = lax.all_to_all(spectra, "sector", split_axis=2, concat_axis=3, tiled=True)
    segments = banded.shape[1]
    per_sector = banded.shape[2] // 2
    grouped = banded.reshape(blocks, segments, 2, per_sector, total_mics)
    distance = distances(radius, azimuth, total_mics)
    scale = 1.0 / (total_mics * blocks * segments * lax.axis_size("blk"))
    flat = grouped.reshape(blocks * segments, 2, per_sector, total_mics)
    partial_power = band_power(flat, sector_index * per_sector, per_sector, distance) * scale
    return lax.psum_scatter(partial_power, "blk", scatter_dimension=0, tiled=True)


def solution(mesh):
    return jax.shard_map(
        local,
        mesh=mesh,
        in_specs=(P("blk", "sector", None), P("blk"), P("blk", None), P(), P()),
        out_specs=P(("sector", "blk"), None),
        check_vma=False,
    )
```

profile of v0, /device:TPU:24, one launch (start us, length us, event | category | flops | bytes accessed | tf_op | source)
XLA Modules:
  0.0 481.5 jit_solution(11197837299432246893)
XLA Ops:
  0.0 2.4 collective-permute-start
  2.4 0.7 fusion.43
  3.1 11.9 %collective-permute-done = bf16[2,32,8192]{2,1,0:T(8,128)(2,1)S(1)} collective-permute-done((bf16[2,32,8192]{2,1,0:T(8,128)(2,1)}, bf16[2,32,8192]{2,1,0:T(8,128)(2,1)S(1)}, u32[]{:S(2)}, u32[]{:S(2)}) %collective-permute-start) | collective-permute-done | bytes 1048608 | tf_op jit(solution)/shard_map/ppermute | solution.py:14
  15.0 1.4 broadcast_select_fusion
  16.5 0.9 collective-permute-start.1
  17.4 23.5 %collective-permute-done.1 = bf16[2,32,8192]{2,1,0:T(8,128)(2,1)S(1)} collective-permute-done((bf16[2,32,8192]{2,1,0:T(8,128)(2,1)S(1)}, bf16[2,32,8192]{2,1,0:T(8,128)(2,1)S(1)}, u32[]{:S(2)}, u32[]{:S(2)}) %collective-permute-start.1) | collective-permute-done | bytes 1048608 | tf_op jit(solution)/shard_map/ppermute | solution.py:14
  41.4 26.4 %collective-permute-done.2 = bf16[2,32,8192]{2,1,0:T(8,128)(2,1)S(1)} collective-permute-done((bf16[2,32,8192]{2,1,0:T(8,128)(2,1)S(1)}, bf16[2,32,8192]{2,1,0:T(8,128)(2,1)S(1)}, u32[]{:S(2)}, u32[]{:S(2)}) %collective-permute-start.2) | collective-permute-done | bytes 1048608 | tf_op jit(solution)/shard_map/ppermute | solution.py:14
  68.0 1.9 collective-permute-start.3
  69.9 23.5 %collective-permute-done.3 = bf16[2,32,8192]{2,1,0:T(8,128)(2,1)S(1)} collective-permute-done((bf16[2,32,8192]{2,1,0:T(8,128)(2,1)S(1)}, bf16[2,32,8192]{2,1,0:T(8,128)(2,1)S(1)}, u32[]{:S(2)}, u32[]{:S(2)}) %collective-permute-start.3) | collective-permute-done | bytes 1048608 | tf_op jit(solution)/shard_map/ppermute | solution.py:14
  93.5 7.1 %collective-permute-start.4 = (bf16[2,32,8192]{2,1,0:T(8,128)(2,1)S(1)}, bf16[2,32,8192]{2,1,0:T(8,128)(2,1)S(1)}, u32[]{:S(2)}, u32[]{:S(2)}) collective-permute-start(bf16[2,32,8192]{2,1,0:T(8,128)(2,1)S(1)} %broadcast_select_fusion.3), channel_id=1, source_target_pairs={{0,224},{2,226},{4,228},{6,230},{8,232},{10,234},{12,236},{14,238}... | collective-permute-start | bytes 3145736 | tf_op jit(solution)/shard_map/ppermute | solution.py:14
  100.7 21.0 %collective-permute-done.4 = bf16[2,32,8192]{2,1,0:T(8,128)(2,1)S(1)} collective-permute-done((bf16[2,32,8192]{2,1,0:T(8,128)(2,1)S(1)}, bf16[2,32,8192]{2,1,0:T(8,128)(2,1)S(1)}, u32[]{:S(2)}, u32[]{:S(2)}) %collective-permute-start.4) | collective-permute-done | bytes 1048608 | tf_op jit(solution)/shard_map/ppermute | solution.py:14
  121.9 2.3 collective-permute-start.5
  124.2 30.1 %collective-permute-done.5 = bf16[2,32,8192]{2,1,0:T(8,128)(2,1)S(1)} collective-permute-done((bf16[2,32,8192]{2,1,0:T(8,128)(2,1)S(1)}, bf16[2,32,8192]{2,1,0:T(8,128)(2,1)S(1)}, u32[]{:S(2)}, u32[]{:S(2)}) %collective-permute-start.5) | collective-permute-done | bytes 1048608 | tf_op jit(solution)/shard_map/ppermute | solution.py:14
  154.4 1.8 collective-permute-start.6
  156.3 46.5 %collective-permute-done.6 = bf16[2,32,8192]{2,1,0:T(8,128)(2,1)S(1)} collective-permute-done((bf16[2,32,8192]{2,1,0:T(8,128)(2,1)S(1)}, bf16[2,32,8192]{2,1,0:T(8,128)(2,1)S(1)}, u32[]{:S(2)}, u32[]{:S(2)}) %collective-permute-start.6) | collective-permute-done | bytes 1048608 | tf_op jit(solution)/shard_map/ppermute | solution.py:14
  202.9 10.8 %collective-permute-start.7 = (bf16[2,32,8192]{2,1,0:T(8,128)(2,1)S(1)}, bf16[2,32,8192]{2,1,0:T(8,128)(2,1)}, u32[]{:S(2)}, u32[]{:S(2)}) collective-permute-start(bf16[2,32,8192]{2,1,0:T(8,128)(2,1)S(1)} %broadcast_select_fusion.6), channel_id=1, source_target_pairs={{0,254},{2,0},{4,2},{6,4},{8,6},{10,8},{12,10},{14,12},{16,14},{18... | collective-permute-start | bytes 3145736 | tf_op jit(solution)/shard_map/ppermute | solution.py:14
  213.9 18.0 %multiply_convert_fusion = bf16[1024,1024]{1,0:T(8,128)(2,1)} fusion(f32[1024]{0:T(1024)S(1)} %multiply_subtract_fusion, s32[1024]{0:T(1024)S(1)} %fusion.40, pred[1024]{0:T(1024)(128)(4,1)S(1)} %fusion.37), kind=kLoop, calls=%fused_computation.32 | loop fusion | flops 19922944 | bytes 2106368 | tf_op jit(solution)/shard_map/convert_element_type | solution.py:30
  232.0 1.4 pad_maximum_fusion
  233.3 5.4 %while.12 = (s32[]{:T(128)}, bf16[2,64,8192]{2,1,0:T(8,128)(2,1)S(1)}, s32[2,3]{1,0:T(2,128)S(1)}, bf16[2,33,8192]{2,1,0:T(8,128)(2,1)}, s32[]{:T(128)}) while((s32[]{:T(128)}, bf16[2,64,8192]{2,1,0:T(8,128)(2,1)S(1)}, s32[2,3]{1,0:T(2,128)S(1)}, bf16[2,33,8192]{2,1,0:T(8,128)(2,1)}, s32[]{:T(128)}) %tuple.63), condition=%wide.while_cond, body=%wide.while_body.sunk | while | flops 2 | bytes 1197673 | solution.py:103
  233.9 2.1 dynamic-slice_dynamic-update-slice_fusion.2
  236.6 2.1 dynamic-slice_dynamic-update-slice_fusion.2
  238.7 2.3 add_convert_fusion.1
  241.9 1.4 fusion.25
  243.3 1.5 fusion.24
  244.7 12.1 %copy.31 = bf16[2,15,1024,32]{3,0,1,2:T(2,128)(2,1)} copy(bf16[2,15,1024,32]{2,3,1,0:T(8,128)(2,1)S(1)} %fusion.24) | data formatting | bytes 3932160 | tf_op jit(solution)/shard_map/convert_element_type | solution.py:70
  256.8 16.9 %reshape.173 = bf16[128,2,3840]{2,1,0:T(2,128)(2,1)} reshape(bf16[1024,15,2,32]{3,2,1,0:T(2,128)(2,1)} %bitcast.50) | data formatting | bytes 3932160
  273.7 22.3 %all-to-all-start = ((bf16[128,2,3840]{2,1,0:T(2,128)(2,1)}), bf16[128,2,3840]{2,1,0:T(2,128)(2,1)S(1)}, u32[]{:S(2)}, u32[]{:S(2)}) async-start(bf16[128,2,3840]{2,1,0:T(2,128)(2,1)} %reshape.173), calls=%async_computation | async-start | bytes 3932160 | tf_op jit(solution)/shard_map/all_to_all | solution.py:108
  297.4 47.4 %all-to-all-done = bf16[128,2,3840]{2,1,0:T(2,128)(2,1)S(1)} async-done(((bf16[128,2,3840]{2,1,0:T(2,128)(2,1)}), bf16[128,2,3840]{2,1,0:T(2,128)(2,1)S(1)}, u32[]{:S(2)}, u32[]{:S(2)}) %all-to-all-start) | async-done | bytes 1966112 | tf_op jit(solution)/shard_map/all_to_all | solution.py:108
  344.9 6.6 %reshape.174 = bf16[1024,15,2,32]{3,2,1,0:T(2,128)(2,1)} reshape(bf16[128,2,3840]{2,1,0:T(2,128)(2,1)S(1)} %all-to-all-done) | data formatting | bytes 3932160
  351.4 5.0 %copy.49 = bf16[2,15,1024,32]{3,2,1,0:T(8,128)(2,1)S(1)} copy(bf16[2,15,1024,32]{3,0,1,2:T(2,128)(2,1)} %bitcast.51) | data formatting | bytes 3932160 | tf_op jit(solution)/shard_map/all_to_all | solution.py:108
  356.4 5.4 %copy.33 = bf16[2,15,8,128,32]{4,3,2,1,0:T(8,128)(2,1)} copy(bf16[2,15,8,128,32]{4,2,3,1,0:T(8,128)(2,1)S(1)} %bitcast.52) | data formatting | bytes 3932160 | tf_op jit(solution)/shard_map/all_to_all | solution.py:108
  361.9 11.3 %reshape_reshape.3 = bf16[30,2,4,4096]{3,2,1,0:T(4,128)(2,1)} reshape(bf16[2,15,8,128,32]{4,3,2,1,0:T(8,128)(2,1)} %copy.33) | data formatting | bytes 3932160 | tf_op jit(solution)/shard_map/reshape;reshape | solution.py:114
  373.2 3.6 copy.34
  376.8 97.6 %while.13 = (s32[]{:T(128)}, f32[4,256]{1,0:T(4,128)S(1)}, s32[4]{0:T(128)S(1)}, bf16[30,2,4,4096]{3,1,0,2:T(2,128)(2,1)S(1)}, s32[]{:T(128)}, /*index=5*/f32[25...) while((s32[]{:T(128)}, f32[4,256]{1,0:T(4,128)S(1)}, ...), condition=%wide.region_2.3_spmd.clone, body=%wide.region_0.2_spmd.clone.sunk | while | flops 269464320 | bytes 12114143 | solution.py:86
  379.7 1.1 fusion.71
  382.0 18.4 %fusion.70 = (bf16[4096,256]{1,0:T(8,128)(2,1)S(1)}, bf16[4096,256]{1,0:T(8,128)(2,1)S(1)}) fusion(f32[256]{0:T(256)S(1)} %get-tuple-element.336, f32[4096]{0:T(1024)S(1)} %get-tuple-element.337, f32[256]{0:T(256)S(1)} %get-tuple-element.334, f32[4096]{0:T(1024)S(1)} %get-tuple-element.335, f32[256]{0:T(256)S(1)} %get-tuple-element.338, f32[]{:T(128)S(6)} %mul.373), kind=kLoop, calls=%fused_computation.10.clone.1 | loop fusion | flops 8388608 | bytes 4230148 | tf_op jit(solution)/shard_map/convert
  400.4 0.7 fusion.72
  401.2 0.6 dynamic_slice.14
  404.1 1.1 fusion.71
  406.4 18.4 %fusion.70 = (bf16[4096,256]{1,0:T(8,128)(2,1)S(1)}, bf16[4096,256]{1,0:T(8,128)(2,1)S(1)}) fusion(f32[256]{0:T(256)S(1)} %get-tuple-element.336, f32[4096]{0:T(1024)S(1)} %get-tuple-element.337, f32[256]{0:T(256)S(1)} %get-tuple-element.334, f32[4096]{0:T(1024)S(1)} %get-tuple-element.335, f32[256]{0:T(256)S(1)} %get-tuple-element.338, f32[]{:T(128)S(6)} %mul.373), kind=kLoop, calls=%fused_computation.10.clone.1 | loop fusion | flops 8388608 | bytes 4230148 | tf_op jit(solution)/shard_map/convert
  424.8 0.7 fusion.72
  428.5 1.1 fusion.71
  430.8 18.4 %fusion.70 = (bf16[4096,256]{1,0:T(8,128)(2,1)S(1)}, bf16[4096,256]{1,0:T(8,128)(2,1)S(1)}) fusion(f32[256]{0:T(256)S(1)} %get-tuple-element.336, f32[4096]{0:T(1024)S(1)} %get-tuple-element.337, f32[256]{0:T(256)S(1)} %get-tuple-element.334, f32[4096]{0:T(1024)S(1)} %get-tuple-element.335, f32[256]{0:T(256)S(1)} %get-tuple-element.338, f32[]{:T(128)S(6)} %mul.373), kind=kLoop, calls=%fused_computation.10.clone.1 | loop fusion | flops 8388608 | bytes 4230148 | tf_op jit(solution)/shard_map/convert
  449.2 0.7 fusion.72
  452.9 1.1 fusion.71
  455.2 18.4 %fusion.70 = (bf16[4096,256]{1,0:T(8,128)(2,1)S(1)}, bf16[4096,256]{1,0:T(8,128)(2,1)S(1)}) fusion(f32[256]{0:T(256)S(1)} %get-tuple-element.336, f32[4096]{0:T(1024)S(1)} %get-tuple-element.337, f32[256]{0:T(256)S(1)} %get-tuple-element.334, f32[4096]{0:T(1024)S(1)} %get-tuple-element.335, f32[256]{0:T(256)S(1)} %get-tuple-element.338, f32[]{:T(128)S(6)} %mul.373), kind=kLoop, calls=%fused_computation.10.clone.1 | loop fusion | flops 8388608 | bytes 4230148 | tf_op jit(solution)/shard_map/convert
  473.6 0.7 fusion.72
  474.4 6.4 %all-reduce.1 = f32[4,256]{1,0:T(4,128)S(1)} all-reduce(f32[4,256]{1,0:T(4,128)S(1)} %broadcast_multiply_fusion), channel_id=2, replica_groups=mesh['sector'=128,'blk'=2] {'blk'}, use_global_device_ids=true, to_apply=%region_3.4.clone | all-reduce | flops 1024 | bytes 8192
  (62 shorter events, 10.8 us)
Async XLA Ops:
  0.0 15.0 %collective-permute-start = (bf16[2,32,8192]{2,1,0:T(8,128)(2,1)}, bf16[2,32,8192]{2,1,0:T(8,128)(2,1)S(1)}, u32[]{:S(2)}, u32[]{:S(2)}) collective-permute-start(bf16[2,32,8192]{2,1,0:T(8,128)(2,1)} %param.7), channel_id=1, source_target_pairs={{0,254},{2,0},{4,2},{6,4},{8,6},{10,8},{12,10},{14,12},{16,14},{18... | collective-permute-start | bytes 3145736 | tf_op jit(solution)/shard_map/ppermute | solution.py:14
  16.5 24.4 %collective-permute-start.1 = (bf16[2,32,8192]{2,1,0:T(8,128)(2,1)S(1)}, bf16[2,32,8192]{2,1,0:T(8,128)(2,1)S(1)}, u32[]{:S(2)}, u32[]{:S(2)}) collective-permute-start(bf16[2,32,8192]{2,1,0:T(8,128)(2,1)S(1)} %broadcast_select_fusion), channel_id=1, source_target_pairs={{0,252},{2,254},{4,0},{6,2},{8,4},{10,6},{12,8},{14,10},{16,12},{1... | collective-permute-start | bytes 3145736 | tf_op jit(solution)/shard_map/ppermute | solution.py:14
  41.1 26.8 %collective-permute-start.2 = (bf16[2,32,8192]{2,1,0:T(8,128)(2,1)S(1)}, bf16[2,32,8192]{2,1,0:T(8,128)(2,1)S(1)}, u32[]{:S(2)}, u32[]{:S(2)}) collective-permute-start(bf16[2,32,8192]{2,1,0:T(8,128)(2,1)S(1)} %broadcast_select_fusion.1), channel_id=1, source_target_pairs={{0,248},{2,250},{4,252},{6,254},{8,0},{10,2},{12,4},{14,6},{16,8},... | collective-permute-start | bytes 3145736 | tf_op jit(solution)/shard_map/ppermute | solution.py:14
  67.9 56.3 %copy-start.3 = (s32[2]{0:T(128)S(1)}, s32[2]{0:T(128)}, u32[]{:S(2)}) copy-start(s32[2]{0:T(128)} %param.8) | copy-start | bytes 28
  68.0 25.3 %collective-permute-start.3 = (bf16[2,32,8192]{2,1,0:T(8,128)(2,1)S(1)}, bf16[2,32,8192]{2,1,0:T(8,128)(2,1)S(1)}, u32[]{:S(2)}, u32[]{:S(2)}) collective-permute-start(bf16[2,32,8192]{2,1,0:T(8,128)(2,1)S(1)} %broadcast_select_fusion.2), channel_id=1, source_target_pairs={{0,240},{2,242},{4,244},{6,246},{8,248},{10,250},{12,252},{14,254}... | collective-permute-start | bytes 3145736 | tf_op jit(solution)/shard_map/ppermute | solution.py:14
  93.4 62.9 %copy-start = (f32[2,8192]{1,0:T(2,128)S(1)}, f32[2,8192]{1,0:T(2,128)}, u32[]{:S(2)}) copy-start(f32[2,8192]{1,0:T(2,128)} %param.9) | copy-start | bytes 196612
  93.5 28.2 %collective-permute-start.4 = (bf16[2,32,8192]{2,1,0:T(8,128)(2,1)S(1)}, bf16[2,32,8192]{2,1,0:T(8,128)(2,1)S(1)}, u32[]{:S(2)}, u32[]{:S(2)}) collective-permute-start(bf16[2,32,8192]{2,1,0:T(8,128)(2,1)S(1)} %broadcast_select_fusion.3), channel_id=1, source_target_pairs={{0,224},{2,226},{4,228},{6,230},{8,232},{10,234},{12,236},{14,238}... | collective-permute-start | bytes 3145736 | tf_op jit(solution)/shard_map/ppermute | solution.py:14
  121.9 32.4 %collective-permute-start.5 = (bf16[2,32,8192]{2,1,0:T(8,128)(2,1)S(1)}, bf16[2,32,8192]{2,1,0:T(8,128)(2,1)S(1)}, u32[]{:S(2)}, u32[]{:S(2)}) collective-permute-start(bf16[2,32,8192]{2,1,0:T(8,128)(2,1)S(1)} %broadcast_select_fusion.4), channel_id=1, source_target_pairs={{0,192},{2,194},{4,196},{6,198},{8,200},{10,202},{12,204},{14,206}... | collective-permute-start | bytes 3145736 | tf_op jit(solution)/shard_map/ppermute | solution.py:14
  154.4 48.4 %collective-permute-start.6 = (bf16[2,32,8192]{2,1,0:T(8,128)(2,1)S(1)}, bf16[2,32,8192]{2,1,0:T(8,128)(2,1)S(1)}, u32[]{:S(2)}, u32[]{:S(2)}) collective-permute-start(bf16[2,32,8192]{2,1,0:T(8,128)(2,1)S(1)} %broadcast_select_fusion.5), channel_id=1, source_target_pairs={{0,128},{2,130},{4,132},{6,134},{8,136},{10,138},{12,140},{14,142}... | collective-permute-start | bytes 3145736 | tf_op jit(solution)/shard_map/ppermute | solution.py:14
  202.9 29.0 %collective-permute-start.7 = (bf16[2,32,8192]{2,1,0:T(8,128)(2,1)S(1)}, bf16[2,32,8192]{2,1,0:T(8,128)(2,1)}, u32[]{:S(2)}, u32[]{:S(2)}) collective-permute-start(bf16[2,32,8192]{2,1,0:T(8,128)(2,1)S(1)} %broadcast_select_fusion.6), channel_id=1, source_target_pairs={{0,254},{2,0},{4,2},{6,4},{8,6},{10,8},{12,10},{14,12},{16,14},{18... | collective-permute-start | bytes 3145736 | tf_op jit(solution)/shard_map/ppermute | solution.py:14
  238.7 3.2 copy-start.5
  256.8 39.2 %copy-start.4 = (u32[256]{0:T(256)S(1)}, u32[256]{0:T(256)}, u32[]{:S(2)}) copy-start(u32[256]{0:T(256)} %constant.255) | copy-start | bytes 3076
  256.8 40.5 %copy-start.1 = (f32[256]{0:T(256)S(1)}, f32[256]{0:T(256)}, u32[]{:S(2)}) copy-start(f32[256]{0:T(256)} %param.10) | copy-start | bytes 3076
  256.8 40.5 %copy-start.2 = (f32[256]{0:T(256)S(1)}, f32[256]{0:T(256)}, u32[]{:S(2)}) copy-start(f32[256]{0:T(256)} %param.11) | copy-start | bytes 3076
  273.7 71.1 %all-to-all-start = ((bf16[128,2,3840]{2,1,0:T(2,128)(2,1)}), bf16[128,2,3840]{2,1,0:T(2,128)(2,1)S(1)}, u32[]{:S(2)}, u32[]{:S(2)}) async-start(bf16[128,2,3840]{2,1,0:T(2,128)(2,1)} %reshape.173), calls=%async_computation | async-start | bytes 3932160 | tf_op jit(solution)/shard_map/all_to_all | solution.py:108
where the time goes:
time: 482 us; the launch traced here: 481 us
  waiting for transfers between devices  230 us (48%)
  other arithmetic  98.7 us (20%)
  local copies, waits for them, and re-layouts  79.3 us (16%)
  starting transfers between devices  49.8 us (10%)
  loops' own time  10.3 us (2%)
  blocking collectives  6.45 us (1%)
  matrix products  5.78 us (1%)
    ppermute x8, waiting for transfers between devices, from_behind(): return lax.ppermute(x, axis, [(i, (i + by) % size) for i in range(size)])  183 us
    another operation x4, other arithmetic  73.4 us
    all_to_all x1, waiting for transfers between devices, local(): lax.all_to_all(spectra, 'sector', split_axis=2, concat_axis=3, tiled=True)  47.4 us
    unnamed x20, local copies, waits for them, and re-layouts  28.7 us
    ppermute x8, starting transfers between devices, from_behind(): return lax.ppermute(x, axis, [(i, (i + by) % size) for i in range(size)])  27.6 us
    all_to_all x1, starting transfers between devices, local(): lax.all_to_all(spectra, 'sector', split_axis=2, concat_axis=3, tiled=True)  22.3 us
    convert_element_type x1, other arithmetic, fourier_table(): return (value * window / math.sqrt(3.0 * NFFT / 8.0)).astype(jnp.bfloat16)  18 us
    convert_element_type x1, local copies, waits for them, and re-layouts, segment_spectra(): return (upper + lower).astype(jnp.bfloat16)  12.1 us
  transfers between devices with their start and end apart: 9, of which 8 were waited for; matrix products, arithmetic and copies ran while one was open for 4% of the time, Pallas kernels for 0%

commit v1 on v0

--- a/solution.py
+++ b/solution.py
@@ -7,6 +7,12 @@
 NFFT = 1024
 wavenumber = 2.0
 height = 0.5
+
+
+def stacked_exchange(value, axis, split, join):
+    pieces = jnp.split(value, lax.axis_size(axis), axis=split)
+    received = lax.all_to_all(jnp.stack(pieces), axis, 0, 0)
+    return jnp.concatenate(received, axis=join)
 
 
 def from_behind(x, axis, by):
@@ -105,7 +111,7 @@
     )
     virtual = interpolate(window_rows, fraction)
     spectra = segment_spectra(virtual, fourier_table(sectors))
-    banded = lax.all_to_all(spectra, "sector", split_axis=2, concat_axis=3, tiled=True)
+    banded = stacked_exchange(spectra, "sector", 2, 3)
     segments = banded.shape[1]
     per_sector = banded.shape[2] // 2
     grouped = banded.reshape(blocks, segments, 2, per_sector, total_mics)

time: 482 us -> 608 us (1.26); the launches traced: 481 us -> 599 us
  local copies, waits for them, and re-layouts: 79.3 us -> 193 us
    unnamed x20 -> x143, local copies, waits for them, and re-layouts: 28.7 us -> 130 us
    another operation x0 -> x2, local copies, waits for them, and re-layouts: none -> 26.2 us  [stacked_exchange(): received = lax.all_to_all(jnp.stack(pieces), axis, 0, 0)]
    convert_element_type x1 -> x0, local copies, waits for them, and re-layouts: 12.1 us -> none  [segment_spectra(): return (upper + lower).astype(jnp.bfloat16)]
    all_to_all x2 -> x0, local copies, waits for them, and re-layouts: 10.4 us -> none  [local(): lax.all_to_all(spectra, 'sector', split_axis=2, concat_axis=3, tiled=True)]
    reshape x0 -> x1, local copies, waits for them, and re-layouts: none -> 8.62 us  [stacked_exchange(): return jnp.concatenate(received, axis=join)]
where the time goes in v1:
time: 608 us; the launch traced here: 599 us
  waiting for transfers between devices  229 us (38%)
  local copies, waits for them, and re-layouts  193 us (32%)
  other arithmetic  100 us (16%)
  starting transfers between devices  49.6 us (8%)
  loops' own time  11.8 us (2%)
  matrix products  8.23 us (1%)
  blocking collectives  6.45 us (1%)
    ppermute x8, waiting for transfers between devices, from_behind(): return lax.ppermute(x, axis, [(i, (i + by) % size) for i in range(size)])  181 us
    unnamed x143, local copies, waits for them, and re-layouts  130 us
    another operation x4, other arithmetic  73.4 us
    all_to_all x1, waiting for transfers between devices, stacked_exchange(): received = lax.all_to_all(jnp.stack(pieces), axis, 0, 0)  47.4 us
    ppermute x8, starting transfers between devices, from_behind(): return lax.ppermute(x, axis, [(i, (i + by) % size) for i in range(size)])  27.4 us
    another operation x2, local copies, waits for them, and re-layouts, stacked_exchange(): received = lax.all_to_all(jnp.stack(pieces), axis, 0, 0)  26.2 us
    all_to_all x1, starting transfers between devices, stacked_exchange(): received = lax.all_to_all(jnp.stack(pieces), axis, 0, 0)  22.3 us
    convert_element_type x1, other arithmetic, fourier_table(): return (value * window / math.sqrt(3.0 * NFFT / 8.0)).astype(jnp.bfloat16)  18.1 us
  transfers between devices with their start and end apart: 9, of which 8 were waited for; matrix products, arithmetic and copies ran while one was open for 4% of the time, Pallas kernels for 0%

profile of v1, /device:TPU:24, one launch (start us, length us, event | category | flops | bytes accessed | tf_op | source)
XLA Modules:
  0.0 599.4 jit_solution(9747245441512234913)
XLA Ops:
  0.0 2.4 collective-permute-start
  3.1 11.9 %collective-permute-done = bf16[2,32,8192]{2,1,0:T(8,128)(2,1)S(1)} collective-permute-done((bf16[2,32,8192]{2,1,0:T(8,128)(2,1)}, bf16[2,32,8192]{2,1,0:T(8,128)(2,1)S(1)}, u32[]{:S(2)}, u32[]{:S(2)}) %collective-permute-start) | collective-permute-done | bytes 1048608 | tf_op jit(solution)/shard_map/ppermute | solution.py:20
  15.0 1.4 broadcast_select_fusion
  16.5 0.9 collective-permute-start.1
  17.4 23.5 %collective-permute-done.1 = bf16[2,32,8192]{2,1,0:T(8,128)(2,1)S(1)} collective-permute-done((bf16[2,32,8192]{2,1,0:T(8,128)(2,1)S(1)}, bf16[2,32,8192]{2,1,0:T(8,128)(2,1)S(1)}, u32[]{:S(2)}, u32[]{:S(2)}) %collective-permute-start.1) | collective-permute-done | bytes 1048608 | tf_op jit(solution)/shard_map/ppermute | solution.py:20
  41.4 26.4 %collective-permute-done.2 = bf16[2,32,8192]{2,1,0:T(8,128)(2,1)S(1)} collective-permute-done((bf16[2,32,8192]{2,1,0:T(8,128)(2,1)S(1)}, bf16[2,32,8192]{2,1,0:T(8,128)(2,1)S(1)}, u32[]{:S(2)}, u32[]{:S(2)}) %collective-permute-start.2) | collective-permute-done | bytes 1048608 | tf_op jit(solution)/shard_map/ppermute | solution.py:20
  68.0 1.9 collective-permute-start.3
  69.9 23.5 %collective-permute-done.3 = bf16[2,32,8192]{2,1,0:T(8,128)(2,1)S(1)} collective-permute-done((bf16[2,32,8192]{2,1,0:T(8,128)(2,1)S(1)}, bf16[2,32,8192]{2,1,0:T(8,128)(2,1)S(1)}, u32[]{:S(2)}, u32[]{:S(2)}) %collective-permute-start.3) | collective-permute-done | bytes 1048608 | tf_op jit(solution)/shard_map/ppermute | solution.py:20
  93.5 7.1 %collective-permute-start.4 = (bf16[2,32,8192]{2,1,0:T(8,128)(2,1)S(1)}, bf16[2,32,8192]{2,1,0:T(8,128)(2,1)S(1)}, u32[]{:S(2)}, u32[]{:S(2)}) collective-permute-start(bf16[2,32,8192]{2,1,0:T(8,128)(2,1)S(1)} %broadcast_select_fusion.3), channel_id=1, source_target_pairs={{0,224},{2,226},{4,228},{6,230},{8,232},{10,234},{12,236},{14,238}... | collective-permute-start | bytes 3145736 | tf_op jit(solution)/shard_map/ppermute | solution.py:20
  100.7 21.0 %collective-permute-done.4 = bf16[2,32,8192]{2,1,0:T(8,128)(2,1)S(1)} collective-permute-done((bf16[2,32,8192]{2,1,0:T(8,128)(2,1)S(1)}, bf16[2,32,8192]{2,1,0:T(8,128)(2,1)S(1)}, u32[]{:S(2)}, u32[]{:S(2)}) %collective-permute-start.4) | collective-permute-done | bytes 1048608 | tf_op jit(solution)/shard_map/ppermute | solution.py:20
  121.9 2.3 collective-permute-start.5
  124.8 29.4 %collective-permute-done.5 = bf16[2,32,8192]{2,1,0:T(8,128)(2,1)S(1)} collective-permute-done((bf16[2,32,8192]{2,1,0:T(8,128)(2,1)S(1)}, bf16[2,32,8192]{2,1,0:T(8,128)(2,1)S(1)}, u32[]{:S(2)}, u32[]{:S(2)}) %collective-permute-start.5) | collective-permute-done | bytes 1048608 | tf_op jit(solution)/shard_map/ppermute | solution.py:20
  154.4 1.8 collective-permute-start.6
  156.2 0.9 broadcast_subtract_fusion
  157.1 45.7 %collective-permute-done.6 = bf16[2,32,8192]{2,1,0:T(8,128)(2,1)S(1)} collective-permute-done((bf16[2,32,8192]{2,1,0:T(8,128)(2,1)S(1)}, bf16[2,32,8192]{2,1,0:T(8,128)(2,1)S(1)}, u32[]{:S(2)}, u32[]{:S(2)}) %collective-permute-start.6) | collective-permute-done | bytes 1048608 | tf_op jit(solution)/shard_map/ppermute | solution.py:20
  202.9 10.6 %collective-permute-start.7 = (bf16[2,32,8192]{2,1,0:T(8,128)(2,1)S(1)}, bf16[2,32,8192]{2,1,0:T(8,128)(2,1)}, u32[]{:S(2)}, u32[]{:S(2)}) collective-permute-start(bf16[2,32,8192]{2,1,0:T(8,128)(2,1)S(1)} %broadcast_select_fusion.6), channel_id=1, source_target_pairs={{0,254},{2,0},{4,2},{6,4},{8,6},{10,8},{12,10},{14,12},{16,14},{18... | collective-permute-start | bytes 3145736 | tf_op jit(solution)/shard_map/ppermute | solution.py:20
  213.7 18.1 %multiply_convert_fusion = bf16[1024,1024]{1,0:T(8,128)(2,1)} fusion(f32[1024]{0:T(1024)S(1)} %multiply_subtract_fusion, s32[1024]{0:T(1024)S(1)} %fusion.40, pred[1024]{0:T(1024)(128)(4,1)S(1)} %fusion.37), kind=kLoop, calls=%fused_computation.31 | loop fusion | flops 19922944 | bytes 2106368 | tf_op jit(solution)/shard_map/convert_element_type | solution.py:36
  231.8 1.4 pad_maximum_fusion
  233.2 6.4 %while.12 = (s32[]{:T(128)}, bf16[2,64,8192]{2,1,0:T(8,128)(2,1)S(1)}, s32[2,3]{1,0:T(2,128)S(1)}, bf16[2,33,8192]{2,1,0:T(8,128)(2,1)}, s32[]{:T(128)}) while((s32[]{:T(128)}, bf16[2,64,8192]{2,1,0:T(8,128)(2,1)S(1)}, s32[2,3]{1,0:T(2,128)S(1)}, bf16[2,33,8192]{2,1,0:T(8,128)(2,1)}, s32[]{:T(128)}) %tuple.63), condition=%wide.while_cond, body=%wide.while_body.sunk | while | flops 2 | bytes 1197673 | solution.py:109
  233.8 2.3 dynamic-slice_dynamic-update-slice_fusion.2
  236.8 2.3 dynamic-slice_dynamic-update-slice_fusion.2
  239.6 2.2 add_convert_fusion.1
  242.6 2.6 fusion.25
  245.2 2.7 fusion.24
  277.1 0.9 constant_dynamic-update-slice_fusion.92
  277.9 0.9 constant_dynamic-update-slice_fusion.91
  297.2 1.0 constant_dynamic-update-slice_fusion.68
  314.0 0.9 constant_dynamic-update-slice_fusion.48
  322.3 0.9 constant_dynamic-update-slice_fusion.38
  333.1 0.9 constant_dynamic-update-slice_fusion.25
  354.9 25.3 %copy.155 = bf16[128,2,15,8,32]{4,3,2,1,0:T(8,128)(2,1)} copy(bf16[128,2,15,8,32]{3,4,2,1,0:T(8,128)(2,1)} %constant_dynamic-update-slice_fusion) | data formatting | bytes 3932160 | tf_op jit(solution)/shard_map/stack | solution.py:14
  380.2 11.7 %reshape.176 = bf16[128,2,3840]{2,1,0:T(2,128)(2,1)} reshape(bf16[128,2,15,8,32]{4,3,2,1,0:T(8,128)(2,1)} %copy.155) | data formatting | bytes 3932160
  391.9 22.3 %all-to-all-start = ((bf16[128,2,3840]{2,1,0:T(2,128)(2,1)}), bf16[128,2,3840]{2,1,0:T(2,128)(2,1)S(1)}, u32[]{:S(2)}, u32[]{:S(2)}) async-start(bf16[128,2,3840]{2,1,0:T(2,128)(2,1)} %reshape.176), calls=%async_computation | async-start | bytes 3932160 | tf_op jit(solution)/shard_map/all_to_all | solution.py:14
  415.7 47.4 %all-to-all-done = bf16[128,2,3840]{2,1,0:T(2,128)(2,1)S(1)} async-done(((bf16[128,2,3840]{2,1,0:T(2,128)(2,1)}), bf16[128,2,3840]{2,1,0:T(2,128)(2,1)S(1)}, u32[]{:S(2)}, u32[]{:S(2)}) %all-to-all-start) | async-done | bytes 1966112 | tf_op jit(solution)/shard_map/all_to_all | solution.py:14
  463.0 6.7 %reshape.177 = bf16[128,2,15,8,32]{4,3,2,1,0:T(8,128)(2,1)} reshape(bf16[128,2,3840]{2,1,0:T(2,128)(2,1)S(1)} %all-to-all-done) | data formatting | bytes 3932160
  469.7 8.6 %copy.156 = bf16[2,15,8,128,32]{4,3,2,1,0:T(8,128)(2,1)} copy(bf16[2,15,8,128,32]{4,2,1,0,3:T(8,128)(2,1)} %bitcast.556) | data formatting | bytes 3932160 | tf_op jit(solution)/shard_map/reshape | solution.py:15
  478.3 11.3 %reshape_reshape_reshape.3 = bf16[30,2,4,4096]{3,2,1,0:T(4,128)(2,1)} reshape(bf16[2,15,8,128,32]{4,3,2,1,0:T(8,128)(2,1)} %copy.156) | data formatting | bytes 3932160 | tf_op jit(solution)/shard_map/reshape;reshape;reshape | solution.py:120
  489.7 3.6 copy.157
  493.3 98.9 %while.13 = (s32[]{:T(128)}, f32[4,256]{1,0:T(4,128)S(1)}, s32[4]{0:T(128)S(1)}, bf16[30,2,4,4096]{3,1,0,2:T(2,128)(2,1)S(1)}, s32[]{:T(128)}, /*index=5*/f32[25...) while((s32[]{:T(128)}, f32[4,256]{1,0:T(4,128)S(1)}, ...), condition=%wide.region_2.3_spmd.clone, body=%wide.region_0.2_spmd.clone.sunk | while | flops 269464320 | bytes 12114143 | solution.py:92
  496.4 1.1 fusion.71
  498.8 18.4 %fusion.70 = (bf16[4096,256]{1,0:T(8,128)(2,1)S(1)}, bf16[4096,256]{1,0:T(8,128)(2,1)S(1)}) fusion(f32[256]{0:T(256)S(1)} %get-tuple-element.336, f32[4096]{0:T(1024)S(1)} %get-tuple-element.337, f32[256]{0:T(256)S(1)} %get-tuple-element.334, f32[4096]{0:T(1024)S(1)} %get-tuple-element.335, f32[256]{0:T(256)S(1)} %get-tuple-element.338, f32[]{:T(128)S(6)} %mul.373), kind=kLoop, calls=%fused_computation.10.clone.1 | loop fusion | flops 8388608 | bytes 4230148 | tf_op jit(solution)/shard_map/convert
  521.2 1.1 fusion.71
  523.5 18.4 %fusion.70 = (bf16[4096,256]{1,0:T(8,128)(2,1)S(1)}, bf16[4096,256]{1,0:T(8,128)(2,1)S(1)}) fusion(f32[256]{0:T(256)S(1)} %get-tuple-element.336, f32[4096]{0:T(1024)S(1)} %get-tuple-element.337, f32[256]{0:T(256)S(1)} %get-tuple-element.334, f32[4096]{0:T(1024)S(1)} %get-tuple-element.335, f32[256]{0:T(256)S(1)} %get-tuple-element.338, f32[]{:T(128)S(6)} %mul.373), kind=kLoop, calls=%fused_computation.10.clone.1 | loop fusion | flops 8388608 | bytes 4230148 | tf_op jit(solution)/shard_map/convert
  545.9 1.1 fusion.71
  548.3 18.4 %fusion.70 = (bf16[4096,256]{1,0:T(8,128)(2,1)S(1)}, bf16[4096,256]{1,0:T(8,128)(2,1)S(1)}) fusion(f32[256]{0:T(256)S(1)} %get-tuple-element.336, f32[4096]{0:T(1024)S(1)} %get-tuple-element.337, f32[256]{0:T(256)S(1)} %get-tuple-element.334, f32[4096]{0:T(1024)S(1)} %get-tuple-element.335, f32[256]{0:T(256)S(1)} %get-tuple-element.338, f32[]{:T(128)S(6)} %mul.373), kind=kLoop, calls=%fused_computation.10.clone.1 | loop fusion | flops 8388608 | bytes 4230148 | tf_op jit(solution)/shard_map/convert
  570.6 1.1 fusion.71
  573.0 18.4 %fusion.70 = (bf16[4096,256]{1,0:T(8,128)(2,1)S(1)}, bf16[4096,256]{1,0:T(8,128)(2,1)S(1)}) fusion(f32[256]{0:T(256)S(1)} %get-tuple-element.336, f32[4096]{0:T(1024)S(1)} %get-tuple-element.337, f32[256]{0:T(256)S(1)} %get-tuple-element.334, f32[4096]{0:T(1024)S(1)} %get-tuple-element.335, f32[256]{0:T(256)S(1)} %get-tuple-element.338, f32[]{:T(128)S(6)} %mul.373), kind=kLoop, calls=%fused_computation.10.clone.1 | loop fusion | flops 8388608 | bytes 4230148 | tf_op jit(solution)/shard_map/convert
  592.2 6.4 %all-reduce.1 = f32[4,256]{1,0:T(4,128)S(1)} all-reduce(f32[4,256]{1,0:T(4,128)S(1)} %broadcast_multiply_fusion), channel_id=2, replica_groups=mesh['sector'=128,'blk'=2] {'blk'}, use_global_device_ids=true, to_apply=%region_3.4.clone | all-reduce | flops 1024 | bytes 8192
  (185 shorter events, 117.7 us)
Async XLA Ops:
  0.0 239.6 %copy-start = (f32[2,8192]{1,0:T(2,128)S(1)}, f32[2,8192]{1,0:T(2,128)}, u32[]{:S(2)}) copy-start(f32[2,8192]{1,0:T(2,128)} %param.9) | copy-start | bytes 196612
  0.0 15.0 %collective-permute-start = (bf16[2,32,8192]{2,1,0:T(8,128)(2,1)}, bf16[2,32,8192]{2,1,0:T(8,128)(2,1)S(1)}, u32[]{:S(2)}, u32[]{:S(2)}) collective-permute-start(bf16[2,32,8192]{2,1,0:T(8,128)(2,1)} %param.7), channel_id=1, source_target_pairs={{0,254},{2,0},{4,2},{6,4},{8,6},{10,8},{12,10},{14,12},{16,14},{18... | collective-permute-start | bytes 3145736 | tf_op jit(solution)/shard_map/ppermute | solution.py:20
  16.5 24.4 %collective-permute-start.1 = (bf16[2,32,8192]{2,1,0:T(8,128)(2,1)S(1)}, bf16[2,32,8192]{2,1,0:T(8,128)(2,1)S(1)}, u32[]{:S(2)}, u32[]{:S(2)}) collective-permute-start(bf16[2,32,8192]{2,1,0:T(8,128)(2,1)S(1)} %broadcast_select_fusion), channel_id=1, source_target_pairs={{0,252},{2,254},{4,0},{6,2},{8,4},{10,6},{12,8},{14,10},{16,12},{1... | collective-permute-start | bytes 3145736 | tf_op jit(solution)/shard_map/ppermute | solution.py:20
  41.1 26.8 %collective-permute-start.2 = (bf16[2,32,8192]{2,1,0:T(8,128)(2,1)S(1)}, bf16[2,32,8192]{2,1,0:T(8,128)(2,1)S(1)}, u32[]{:S(2)}, u32[]{:S(2)}) collective-permute-start(bf16[2,32,8192]{2,1,0:T(8,128)(2,1)S(1)} %broadcast_select_fusion.1), channel_id=1, source_target_pairs={{0,248},{2,250},{4,252},{6,254},{8,0},{10,2},{12,4},{14,6},{16,8},... | collective-permute-start | bytes 3145736 | tf_op jit(solution)/shard_map/ppermute | solution.py:20
  68.0 25.3 %collective-permute-start.3 = (bf16[2,32,8192]{2,1,0:T(8,128)(2,1)S(1)}, bf16[2,32,8192]{2,1,0:T(8,128)(2,1)S(1)}, u32[]{:S(2)}, u32[]{:S(2)}) collective-permute-start(bf16[2,32,8192]{2,1,0:T(8,128)(2,1)S(1)} %broadcast_select_fusion.2), channel_id=1, source_target_pairs={{0,240},{2,242},{4,244},{6,246},{8,248},{10,250},{12,252},{14,254}... | collective-permute-start | bytes 3145736 | tf_op jit(solution)/shard_map/ppermute | solution.py:20
  93.5 28.2 %collective-permute-start.4 = (bf16[2,32,8192]{2,1,0:T(8,128)(2,1)S(1)}, bf16[2,32,8192]{2,1,0:T(8,128)(2,1)S(1)}, u32[]{:S(2)}, u32[]{:S(2)}) collective-permute-start(bf16[2,32,8192]{2,1,0:T(8,128)(2,1)S(1)} %broadcast_select_fusion.3), channel_id=1, source_target_pairs={{0,224},{2,226},{4,228},{6,230},{8,232},{10,234},{12,236},{14,238}... | collective-permute-start | bytes 3145736 | tf_op jit(solution)/shard_map/ppermute | solution.py:20
  121.9 32.4 %collective-permute-start.5 = (bf16[2,32,8192]{2,1,0:T(8,128)(2,1)S(1)}, bf16[2,32,8192]{2,1,0:T(8,128)(2,1)S(1)}, u32[]{:S(2)}, u32[]{:S(2)}) collective-permute-start(bf16[2,32,8192]{2,1,0:T(8,128)(2,1)S(1)} %broadcast_select_fusion.4), channel_id=1, source_target_pairs={{0,192},{2,194},{4,196},{6,198},{8,200},{10,202},{12,204},{14,206}... | collective-permute-start | bytes 3145736 | tf_op jit(solution)/shard_map/ppermute | solution.py:20
  154.4 48.4 %collective-permute-start.6 = (bf16[2,32,8192]{2,1,0:T(8,128)(2,1)S(1)}, bf16[2,32,8192]{2,1,0:T(8,128)(2,1)S(1)}, u32[]{:S(2)}, u32[]{:S(2)}) collective-permute-start(bf16[2,32,8192]{2,1,0:T(8,128)(2,1)S(1)} %broadcast_select_fusion.5), channel_id=1, source_target_pairs={{0,128},{2,130},{4,132},{6,134},{8,136},{10,138},{12,140},{14,142}... | collective-permute-start | bytes 3145736 | tf_op jit(solution)/shard_map/ppermute | solution.py:20
  202.9 28.9 %collective-permute-start.7 = (bf16[2,32,8192]{2,1,0:T(8,128)(2,1)S(1)}, bf16[2,32,8192]{2,1,0:T(8,128)(2,1)}, u32[]{:S(2)}, u32[]{:S(2)}) collective-permute-start(bf16[2,32,8192]{2,1,0:T(8,128)(2,1)S(1)} %broadcast_select_fusion.6), channel_id=1, source_target_pairs={{0,254},{2,0},{4,2},{6,4},{8,6},{10,8},{12,10},{14,12},{16,14},{18... | collective-permute-start | bytes 3145736 | tf_op jit(solution)/shard_map/ppermute | solution.py:20
  338.2 76.0 %copy-start.3 = (u32[256]{0:T(256)S(1)}, u32[256]{0:T(256)}, u32[]{:S(2)}) copy-start(u32[256]{0:T(256)} %constant.255) | copy-start | bytes 3076
  338.2 77.4 %copy-start.1 = (f32[256]{0:T(256)S(1)}, f32[256]{0:T(256)}, u32[]{:S(2)}) copy-start(f32[256]{0:T(256)} %param.10) | copy-start | bytes 3076
  338.2 77.5 %copy-start.2 = (f32[256]{0:T(256)S(1)}, f32[256]{0:T(256)}, u32[]{:S(2)}) copy-start(f32[256]{0:T(256)} %param.11) | copy-start | bytes 3076
  391.9 71.1 %all-to-all-start = ((bf16[128,2,3840]{2,1,0:T(2,128)(2,1)}), bf16[128,2,3840]{2,1,0:T(2,128)(2,1)S(1)}, u32[]{:S(2)}, u32[]{:S(2)}) async-start(bf16[128,2,3840]{2,1,0:T(2,128)(2,1)} %reshape.176), calls=%async_computation | async-start | bytes 3932160 | tf_op jit(solution)/shard_map/all_to_all | solution.py:14
